TPU v7x, 128 devices: a whole 4x4x4 slice. The times are simulated.
128 devices in a mesh: row: 32 (over z, x, core), grp: 4 (over y).
Axes of the slice: x: 4, y: 4, z: 4, core: 2. Of those that a mesh axis runs over, the one named last changes fastest.
Arguments:
- features: bfloat16 [262144, 768], P(('row', 'grp')), may hold values from -6 to 6
- dense_edge_weights: bfloat16 [1024, 4, 256, 256], P(('row', 'grp')), may hold values from -0.125 to 0.125
- dense_cols: int32 [1024, 4], P(('row', 'grp')), may hold values from 0 to 7
- dense_ids: int32 [8], replicated, may hold values from 0 to 1023, as said below
- sparse_w: bfloat16 [262144, 1024], P(('row', 'grp')), may hold values from -0.125 to 0.125
- sparse_rows: int32 [128, 128, 8], P(('row', 'grp')), may hold values from 0 to 2047, as said below
- sparse_counts: int32 [128, 128], P(('row', 'grp')), may hold values from 1 to 8, as said below
- weight: bfloat16 [768, 768], replicated, may hold values from -0.21875 to 0.21875
- bias: float32 [768], replicated, may hold values from -3 to 3
Outputs:
- output: bfloat16 [262144, 768], P(('row', 'grp'))
Inputs may be any that keep to these rules, and one draw needn't show every extreme that they name: `dense_ids`: distinct row block ids; the first and the last row block are both among them. `sparse_rows`: local row indices of the sender. `sparse_counts`: at most 8 rows from one sender to one receiver; one receiver gets 8 rows from every sender.
All inputs are finite; a program needn't handle non-finite values.
Results may differ from a plain program's by a relative error of at most 0.0044.
Values may be sent and summed in bfloat16 or wider, within the bound.
A program may use at most 128 MiB of HBM per device.

v0:
```python
import jax
import jax.numpy as jnp
from jax import lax
from jax.sharding import PartitionSpec as P


def from_root(x, axis, root):
    mine = lax.axis_index(axis) == root
    return lax.psum(jnp.where(mine, x, jnp.zeros_like(x)), axis)


def on_device(
    features,
    dense_edge_weights,
    dense_cols,
    dense_ids,
    sparse_w,
    sparse_rows,
    sparse_counts,
    weight,
    bias,
):
    block_count = dense_edge_weights.shape[0]
    tiles_per = dense_edge_weights.shape[1]
    tile_size = dense_edge_weights.shape[2]
    feature_width = features.shape[1]
    stripe_count = dense_ids.shape[0]
    local_blocks = features.reshape(block_count, tile_size, feature_width)

    def fetch_stripe(index, dense_bands):
        global_id = dense_ids[index]
        owner = global_id // block_count
        candidate = lax.dynamic_index_in_dim(
            local_blocks, global_id % block_count, 0, keepdims=False
        )
        arrived = from_root(candidate, ("row", "grp"), owner)
        return lax.dynamic_update_index_in_dim(dense_bands, arrived, index, 0)

    empty_stripes = jnp.zeros((stripe_count, tile_size, feature_width), jnp.bfloat16)
    dense_bands = lax.fori_loop(0, stripe_count, fetch_stripe, empty_stripes)
    dense_sum = jnp.zeros((block_count, tile_size, feature_width), jnp.float32)
    for tile_index in range(tiles_per):
        picked_tiles = dense_bands[dense_cols[:, tile_index]]
        dense_sum = dense_sum + jnp.einsum(
            "eim,emh->eih",
            dense_edge_weights[:, tile_index],
            picked_tiles,
            preferred_element_type=jnp.float32,
        )
    rows_out = sparse_rows[0]
    counts_out = sparse_counts[0]
    peer_count = rows_out.shape[0]
    slot_count = rows_out.shape[1]
    outgoing = features[rows_out]
    slot_ids = jnp.arange(slot_count, dtype=jnp.int32)
    live_slots = slot_ids[None, :] < counts_out[:, None]
    outgoing = jnp.where(live_slots[:, :, None], outgoing, jnp.zeros((), outgoing.dtype))
    arrived_rows = lax.all_to_all(outgoing, ("row", "grp"), split_axis=0, concat_axis=0, tiled=True)
    incoming_rows = arrived_rows.reshape(peer_count * slot_count, feature_width)
    sparse_sum = jnp.dot(sparse_w, incoming_rows, preferred_element_type=jnp.float32)
    aggregate = (dense_sum.reshape(block_count * tile_size, feature_width) + sparse_sum).astype(
        jnp.bfloat16
    )
    result = jnp.dot(aggregate, weight, preferred_element_type=jnp.float32) + bias
    return jnp.maximum(result, 0.0).astype(jnp.bfloat16)


def solution(mesh):
    placed = (
        P(("row", "grp"), None),
        P(("row", "grp"), None, None, None),
        P(("row", "grp"), None),
        P(),
        P(("row", "grp"), None),
        P(("row", "grp"), None, None),
        P(("row", "grp"), None),
        P(),
        P(),
    )
    return jax.shard_map(
        on_device, mesh=mesh, in_specs=placed, out_specs=P(("row", "grp"), None), check_vma=False
    )
```

profile of v0, /device:TPU:1, one launch (start us, length us, event | category | flops | bytes accessed | tf_op | source)
XLA Modules:
  0.0 1288.7 jit_solution(11461242823182639601)
XLA Ops:
  6.5 0.8 compare_select_fusion
  7.5 0.7 iota_compare_fusion
  8.3 6.8 gather_fusion.4
  15.1 1.4 bitcast_select_fusion
  16.5 11.9 all-to-all-start
  28.4 1201.3 %while.15 = (s32[]{:T(128)}, bf16[8,256,768]{2,1,0:T(8,128)(2,1)}, s32[8]{0:T(128)S(1)}, bf16[8,256,768]{2,1,0:T(8,128)(2,1)}, s32[]{:T(128)}, /*index=5*/s32[]{...) while((s32[]{:T(128)}, bf16[8,256,768]{2,1,0:T(8,128)(2,1)}, ...), condition=%wide.region_2.3_spmd, body=%wide.region_0.2_spmd.sunk | while | flops 393248 | bytes 3932668 | solution.py:40
  28.5 0.6 dynamic_slice.25
  31.7 1.8 dynamic-slice_select_fusion.2
  33.5 147.3 %all-reduce.2.cloned.1.call-done = bf16[1,256,768]{2,1,0:T(8,128)(2,1)} async-done(((bf16[1,256,768]{2,1,0:T(8,128)(2,1)}), bf16[1,256,768]{2,1,0:T(8,128)(2,1)}) %all-reduce.2.cloned.1.call-update) | async-done | bytes 393232 | tf_op jit(solution)/shard_map/while/body/eval_jaxpr/psum | solution.py:9
  180.8 1.8 constant_dynamic-update-slice_fusion.2
  182.6 0.6 dynamic_slice.25
  185.8 1.8 dynamic-slice_select_fusion.2
  187.6 143.0 %all-reduce.2.cloned.1.call-done = bf16[1,256,768]{2,1,0:T(8,128)(2,1)} async-done(((bf16[1,256,768]{2,1,0:T(8,128)(2,1)}), bf16[1,256,768]{2,1,0:T(8,128)(2,1)}) %all-reduce.2.cloned.1.call-update) | async-done | bytes 393232 | tf_op jit(solution)/shard_map/while/body/eval_jaxpr/psum | solution.py:9
  330.6 1.8 constant_dynamic-update-slice_fusion.2
  332.3 0.6 dynamic_slice.25
  335.5 1.8 dynamic-slice_select_fusion.2
  337.3 143.0 %all-reduce.2.cloned.1.call-done = bf16[1,256,768]{2,1,0:T(8,128)(2,1)} async-done(((bf16[1,256,768]{2,1,0:T(8,128)(2,1)}), bf16[1,256,768]{2,1,0:T(8,128)(2,1)}) %all-reduce.2.cloned.1.call-update) | async-done | bytes 393232 | tf_op jit(solution)/shard_map/while/body/eval_jaxpr/psum | solution.py:9
  480.3 1.8 constant_dynamic-update-slice_fusion.2
  482.0 0.6 dynamic_slice.25
  485.2 1.8 dynamic-slice_select_fusion.2
  487.0 142.6 %all-reduce.2.cloned.1.call-done = bf16[1,256,768]{2,1,0:T(8,128)(2,1)} async-done(((bf16[1,256,768]{2,1,0:T(8,128)(2,1)}), bf16[1,256,768]{2,1,0:T(8,128)(2,1)}) %all-reduce.2.cloned.1.call-update) | async-done | bytes 393232 | tf_op jit(solution)/shard_map/while/body/eval_jaxpr/psum | solution.py:9
  629.7 1.8 constant_dynamic-update-slice_fusion.2
  631.4 0.6 dynamic_slice.25
  634.6 1.8 dynamic-slice_select_fusion.2
  636.4 142.7 %all-reduce.2.cloned.1.call-done = bf16[1,256,768]{2,1,0:T(8,128)(2,1)} async-done(((bf16[1,256,768]{2,1,0:T(8,128)(2,1)}), bf16[1,256,768]{2,1,0:T(8,128)(2,1)}) %all-reduce.2.cloned.1.call-update) | async-done | bytes 393232 | tf_op jit(solution)/shard_map/while/body/eval_jaxpr/psum | solution.py:9
  779.1 1.8 constant_dynamic-update-slice_fusion.2
  780.8 0.6 dynamic_slice.25
  784.0 1.8 dynamic-slice_select_fusion.2
  785.8 142.6 %all-reduce.2.cloned.1.call-done = bf16[1,256,768]{2,1,0:T(8,128)(2,1)} async-done(((bf16[1,256,768]{2,1,0:T(8,128)(2,1)}), bf16[1,256,768]{2,1,0:T(8,128)(2,1)}) %all-reduce.2.cloned.1.call-update) | async-done | bytes 393232 | tf_op jit(solution)/shard_map/while/body/eval_jaxpr/psum | solution.py:9
  928.5 1.8 constant_dynamic-update-slice_fusion.2
  930.2 0.6 dynamic_slice.25
  933.4 1.8 dynamic-slice_select_fusion.2
  935.2 143.0 %all-reduce.2.cloned.1.call-done = bf16[1,256,768]{2,1,0:T(8,128)(2,1)} async-done(((bf16[1,256,768]{2,1,0:T(8,128)(2,1)}), bf16[1,256,768]{2,1,0:T(8,128)(2,1)}) %all-reduce.2.cloned.1.call-update) | async-done | bytes 393232 | tf_op jit(solution)/shard_map/while/body/eval_jaxpr/psum | solution.py:9
  1078.2 1.8 constant_dynamic-update-slice_fusion.2
  1083.2 1.8 dynamic-slice_select_fusion.2
  1085.0 143.0 %all-reduce.2.cloned.1.call-done = bf16[1,256,768]{2,1,0:T(8,128)(2,1)} async-done(((bf16[1,256,768]{2,1,0:T(8,128)(2,1)}), bf16[1,256,768]{2,1,0:T(8,128)(2,1)}) %all-reduce.2.cloned.1.call-update) | async-done | bytes 393232 | tf_op jit(solution)/shard_map/while/body/eval_jaxpr/psum | solution.py:9
  1227.9 1.8 constant_dynamic-update-slice_fusion.2
  1229.7 4.3 gather_fusion.1
  1234.0 4.3 gather_fusion
  1238.3 6.0 fusion.5
  1244.4 4.8 fusion.7
  1249.2 4.3 gather_fusion.2
  1253.5 4.4 gather_fusion.3
  1257.9 3.3 fusion.3
  1261.3 1.9 slice-done.1
  1263.2 6.7 add_add_fusion
  1269.9 7.9 fusion
  1277.9 4.0 maximum_convert_fusion
  (41 shorter events, 1.1 us)
Async XLA Ops:
  6.5 1271.3 %copy-start = (bf16[768,768]{1,0:T(8,128)(2,1)S(1)}, bf16[768,768]{1,0:T(8,128)(2,1)}, u32[]{:S(2)}) copy-start(bf16[768,768]{1,0:T(8,128)(2,1)} %param.18) | copy-start | bytes 3538948
  15.1 13.3 %copy-start.3 = (s32[8,4]{0,1:T(4,128)S(1)}, s32[8,4]{0,1:T(4,128)}, u32[]{:S(2)}) copy-start(s32[8,4]{0,1:T(4,128)} %param.13) | copy-start | bytes 388
  15.1 13.3 %copy-start.5 = (s32[8]{0:T(128)S(1)}, s32[8]{0:T(128)}, u32[]{:S(2)}) copy-start(s32[8]{0:T(128)} %param.14) | copy-start | bytes 100
  16.5 1253.5 %all-to-all-start = ((bf16[128,8,768]{2,1,0:T(8,128)(2,1)}), bf16[128,8,768]{2,1,0:T(8,128)(2,1)}, u32[]{:S(2)}, u32[]{:S(2)}) async-start(bf16[128,8,768]{2,1,0:T(8,128)(2,1)} %bitcast_select_fusion), calls=%async_computation | async-start | bytes 3145728 | tf_op jit(solution)/shard_map/all_to_all | solution.py:58
  28.4 152.4 %all-reduce.2.cloned.1.call-start = ((), (), s32[]{:S(2)}) async-start(), calls=%async_computation.1 | async-start | bytes 786432 | tf_op jit(solution)/shard_map/while/body/eval_jaxpr/psum | solution.py:9
  182.6 148.0 %all-reduce.2.cloned.1.call-start = ((), (), s32[]{:S(2)}) async-start(), calls=%async_computation.1 | async-start | bytes 786432 | tf_op jit(solution)/shard_map/while/body/eval_jaxpr/psum | solution.py:9
  332.3 147.9 %all-reduce.2.cloned.1.call-start = ((), (), s32[]{:S(2)}) async-start(), calls=%async_computation.1 | async-start | bytes 786432 | tf_op jit(solution)/shard_map/while/body/eval_jaxpr/psum | solution.py:9
  482.0 147.6 %all-reduce.2.cloned.1.call-start = ((), (), s32[]{:S(2)}) async-start(), calls=%async_computation.1 | async-start | bytes 786432 | tf_op jit(solution)/shard_map/while/body/eval_jaxpr/psum | solution.py:9
  631.4 147.6 %all-reduce.2.cloned.1.call-start = ((), (), s32[]{:S(2)}) async-start(), calls=%async_computation.1 | async-start | bytes 786432 | tf_op jit(solution)/shard_map/while/body/eval_jaxpr/psum | solution.py:9
  780.8 147.6 %all-reduce.2.cloned.1.call-start = ((), (), s32[]{:S(2)}) async-start(), calls=%async_computation.1 | async-start | bytes 786432 | tf_op jit(solution)/shard_map/while/body/eval_jaxpr/psum | solution.py:9
  930.2 148.0 %all-reduce.2.cloned.1.call-start = ((), (), s32[]{:S(2)}) async-start(), calls=%async_computation.1 | async-start | bytes 786432 | tf_op jit(solution)/shard_map/while/body/eval_jaxpr/psum | solution.py:9
  1080.0 148.0 %all-reduce.2.cloned.1.call-start = ((), (), s32[]{:S(2)}) async-start(), calls=%async_computation.1 | async-start | bytes 786432 | tf_op jit(solution)/shard_map/while/body/eval_jaxpr/psum | solution.py:9
  1238.3 6.0 copy-start.2
  1253.5 7.8 slice-start
  1257.9 5.3 slice-start.1
  1257.9 5.3 copy-start.1
  1269.9 8.0 copy-start.4
Sparse Core Ops, SparseCore 0:
  34.0 146.8 all-reduce.1
  188.1 142.3 all-reduce.1
  337.8 142.3 all-reduce.1
  487.2 142.3 all-reduce.1
  636.6 142.3 all-reduce.1
  786.0 142.3 all-reduce.1
  935.8 142.3 all-reduce.1
  1085.5 142.3 all-reduce.1
where the time goes:
time: 1290 us
  waiting for transfers between devices  1150 us (89%)
  local copies, waits for them, and re-layouts  45.2 us (4%)
  matrix products  32.9 us (3%)
  loops' own time  20.7 us (2%)
  other arithmetic  17.2 us (1%)
  between operations  13.5 us (1%)
    psum x8, waiting for transfers between devices, from_root(): return lax.psum(jnp.where(mine, x, jnp.zeros_like(x)), axis)  1150 us
  transfers between devices with their start and end apart: 9, of which 8 were waited for; matrix products, arithmetic and copies ran while one was open for 6% of the time, Pallas kernels for 0%

commit v1 on v0

--- a/solution.py
+++ b/solution.py
@@ -6,7 +6,7 @@
 
 def from_root(x, axis, root):
     mine = lax.axis_index(axis) == root
-    return lax.psum(jnp.where(mine, x, jnp.zeros_like(x)), axis)
+    return jnp.sum(lax.all_gather(jnp.where(mine, x, jnp.zeros_like(x)), axis), axis=0)
 
 
 def on_device(

time: 1290 us -> 1350 us (1.047)
  other arithmetic: 17.2 us -> 149 us
  waiting for transfers between devices: 1150 us -> 1080 us
    psum x8 -> x0, waiting for transfers between devices: 1150 us -> none  [from_root(): return lax.psum(jnp.where(mine, x, jnp.zeros_like(x)), axis)]
    all_gather x0 -> x8, waiting for transfers between devices: none -> 1080 us  [from_root(): lax.all_gather(jnp.where(mine, x, jnp.zeros_like(x)), axis)]
    reduce_sum x0 -> x8, other arithmetic: none -> 132 us  [from_root(): jnp.sum(lax.all_gather(jnp.where(mine, x, jnp.zeros_like(x)), axis), axis=0)]
  transfers between devices with their start and end apart: 9 -> 9, of which waited for: 8 -> 8; matrix products, arithmetic and copies ran while one was open for 6% -> 15% of each run, Pallas kernels for 0% -> 0%
where the time goes in v1:
time: 1350 us
  waiting for transfers between devices  1080 us (80%)
  other arithmetic  149 us (11%)
  local copies, waits for them, and re-layouts  44 us (3%)
  matrix products  31.4 us (2%)
  loops' own time  20.7 us (2%)
  between operations  13.5 us (1%)
    all_gather x8, waiting for transfers between devices, from_root(): lax.all_gather(jnp.where(mine, x, jnp.zeros_like(x)), axis)  1080 us
    reduce_sum x8, other arithmetic, from_root(): jnp.sum(lax.all_gather(jnp.where(mine, x, jnp.zeros_like(x)), axis), axis=0)  132 us
  transfers between devices with their start and end apart: 9, of which 8 were waited for; matrix products, arithmetic and copies ran while one was open for 15% of the time, Pallas kernels for 0%

profile of v1, /device:TPU:1, one launch (start us, length us, event | category | flops | bytes accessed | tf_op | source)
XLA Modules:
  0.0 1346.9 jit_solution(2200431450702272886)
XLA Ops:
  6.5 0.8 compare_select_fusion
  8.3 6.8 gather_fusion.4
  15.1 1.4 bitcast_select_fusion
  16.4 11.9 all-to-all-start
  28.4 1254.3 %while.15 = (s32[]{:T(128)}, bf16[8,256,768]{2,1,0:T(8,128)(2,1)}, s32[8]{0:T(128)S(1)}, bf16[8,256,768]{2,1,0:T(8,128)(2,1)}, s32[]{:T(128)}, /*index=5*/s32[]{...) while((s32[]{:T(128)}, bf16[8,256,768]{2,1,0:T(8,128)(2,1)}, ...), condition=%wide.region_2.3_spmd, body=%wide.region_0.2_spmd.sunk | while | flops 25165856 | bytes 204472816 | solution.py:40
  31.6 1.8 dynamic-slice_select_fusion.2
  33.4 136.8 %all-gather.2.cloned.1.call-done = bf16[128,256,768]{2,1,0:T(8,128)(2,1)} async-done(((bf16[1,256,768]{2,1,0:T(8,128)(2,1)}), bf16[128,256,768]{2,1,0:T(8,128)(2,1)}) %all-gather.2.cloned.1.call-update) | async-done | bytes 50331664 | tf_op jit(solution)/shard_map/while/body/eval_jaxpr/all_gather | solution.py:9
  170.3 16.5 %reduce_sum.15 = bf16[256,768]{1,0:T(8,128)(2,1)S(1)} reduce(bf16[128,256,768]{2,1,0:T(8,128)(2,1)} %all-gather.2.cloned.1.call-done, bf16[]{:T(256)} %constant.144.clone.2..sunk), dimensions={0}, to_apply=%region_1.1 | reduce | flops 24969216 | bytes 50724864 | tf_op jit(solution)/shard_map/while/body/eval_jaxpr/reduce_sum | solution.py:9
  186.8 0.8 bitcast_dynamic-update-slice_fusion.2
  190.7 1.8 dynamic-slice_select_fusion.2
  192.5 134.2 %all-gather.2.cloned.1.call-done = bf16[128,256,768]{2,1,0:T(8,128)(2,1)} async-done(((bf16[1,256,768]{2,1,0:T(8,128)(2,1)}), bf16[128,256,768]{2,1,0:T(8,128)(2,1)}) %all-gather.2.cloned.1.call-update) | async-done | bytes 50331664 | tf_op jit(solution)/shard_map/while/body/eval_jaxpr/all_gather | solution.py:9
  326.7 16.5 %reduce_sum.15 = bf16[256,768]{1,0:T(8,128)(2,1)S(1)} reduce(bf16[128,256,768]{2,1,0:T(8,128)(2,1)} %all-gather.2.cloned.1.call-done, bf16[]{:T(256)} %constant.144.clone.2..sunk), dimensions={0}, to_apply=%region_1.1 | reduce | flops 24969216 | bytes 50724864 | tf_op jit(solution)/shard_map/while/body/eval_jaxpr/reduce_sum | solution.py:9
  343.2 0.8 bitcast_dynamic-update-slice_fusion.2
  347.2 1.8 dynamic-slice_select_fusion.2
  349.0 134.2 %all-gather.2.cloned.1.call-done = bf16[128,256,768]{2,1,0:T(8,128)(2,1)} async-done(((bf16[1,256,768]{2,1,0:T(8,128)(2,1)}), bf16[128,256,768]{2,1,0:T(8,128)(2,1)}) %all-gather.2.cloned.1.call-update) | async-done | bytes 50331664 | tf_op jit(solution)/shard_map/while/body/eval_jaxpr/all_gather | solution.py:9
  483.1 16.5 %reduce_sum.15 = bf16[256,768]{1,0:T(8,128)(2,1)S(1)} reduce(bf16[128,256,768]{2,1,0:T(8,128)(2,1)} %all-gather.2.cloned.1.call-done, bf16[]{:T(256)} %constant.144.clone.2..sunk), dimensions={0}, to_apply=%region_1.1 | reduce | flops 24969216 | bytes 50724864 | tf_op jit(solution)/shard_map/while/body/eval_jaxpr/reduce_sum | solution.py:9
  499.7 0.8 bitcast_dynamic-update-slice_fusion.2
  503.6 1.8 dynamic-slice_select_fusion.2
  505.4 134.2 %all-gather.2.cloned.1.call-done = bf16[128,256,768]{2,1,0:T(8,128)(2,1)} async-done(((bf16[1,256,768]{2,1,0:T(8,128)(2,1)}), bf16[128,256,768]{2,1,0:T(8,128)(2,1)}) %all-gather.2.cloned.1.call-update) | async-done | bytes 50331664 | tf_op jit(solution)/shard_map/while/body/eval_jaxpr/all_gather | solution.py:9
  639.6 16.5 %reduce_sum.15 = bf16[256,768]{1,0:T(8,128)(2,1)S(1)} reduce(bf16[128,256,768]{2,1,0:T(8,128)(2,1)} %all-gather.2.cloned.1.call-done, bf16[]{:T(256)} %constant.144.clone.2..sunk), dimensions={0}, to_apply=%region_1.1 | reduce | flops 24969216 | bytes 50724864 | tf_op jit(solution)/shard_map/while/body/eval_jaxpr/reduce_sum | solution.py:9
  656.1 0.8 bitcast_dynamic-update-slice_fusion.2
  660.1 1.8 dynamic-slice_select_fusion.2
  661.9 134.2 %all-gather.2.cloned.1.call-done = bf16[128,256,768]{2,1,0:T(8,128)(2,1)} async-done(((bf16[1,256,768]{2,1,0:T(8,128)(2,1)}), bf16[128,256,768]{2,1,0:T(8,128)(2,1)}) %all-gather.2.cloned.1.call-update) | async-done | bytes 50331664 | tf_op jit(solution)/shard_map/while/body/eval_jaxpr/all_gather | solution.py:9
  796.0 16.5 %reduce_sum.15 = bf16[256,768]{1,0:T(8,128)(2,1)S(1)} reduce(bf16[128,256,768]{2,1,0:T(8,128)(2,1)} %all-gather.2.cloned.1.call-done, bf16[]{:T(256)} %constant.144.clone.2..sunk), dimensions={0}, to_apply=%region_1.1 | reduce | flops 24969216 | bytes 50724864 | tf_op jit(solution)/shard_map/while/body/eval_jaxpr/reduce_sum | solution.py:9
  812.6 0.8 bitcast_dynamic-update-slice_fusion.2
  816.5 1.8 dynamic-slice_select_fusion.2
  818.3 134.2 %all-gather.2.cloned.1.call-done = bf16[128,256,768]{2,1,0:T(8,128)(2,1)} async-done(((bf16[1,256,768]{2,1,0:T(8,128)(2,1)}), bf16[128,256,768]{2,1,0:T(8,128)(2,1)}) %all-gather.2.cloned.1.call-update) | async-done | bytes 50331664 | tf_op jit(solution)/shard_map/while/body/eval_jaxpr/all_gather | solution.py:9
  952.5 16.5 %reduce_sum.15 = bf16[256,768]{1,0:T(8,128)(2,1)S(1)} reduce(bf16[128,256,768]{2,1,0:T(8,128)(2,1)} %all-gather.2.cloned.1.call-done, bf16[]{:T(256)} %constant.144.clone.2..sunk), dimensions={0}, to_apply=%region_1.1 | reduce | flops 24969216 | bytes 50724864 | tf_op jit(solution)/shard_map/while/body/eval_jaxpr/reduce_sum | solution.py:9
  969.0 0.8 bitcast_dynamic-update-slice_fusion.2
  973.0 1.8 dynamic-slice_select_fusion.2
  974.8 134.2 %all-gather.2.cloned.1.call-done = bf16[128,256,768]{2,1,0:T(8,128)(2,1)} async-done(((bf16[1,256,768]{2,1,0:T(8,128)(2,1)}), bf16[128,256,768]{2,1,0:T(8,128)(2,1)}) %all-gather.2.cloned.1.call-update) | async-done | bytes 50331664 | tf_op jit(solution)/shard_map/while/body/eval_jaxpr/all_gather | solution.py:9
  1108.9 16.5 %reduce_sum.15 = bf16[256,768]{1,0:T(8,128)(2,1)S(1)} reduce(bf16[128,256,768]{2,1,0:T(8,128)(2,1)} %all-gather.2.cloned.1.call-done, bf16[]{:T(256)} %constant.144.clone.2..sunk), dimensions={0}, to_apply=%region_1.1 | reduce | flops 24969216 | bytes 50724864 | tf_op jit(solution)/shard_map/while/body/eval_jaxpr/reduce_sum | solution.py:9
  1125.5 0.8 bitcast_dynamic-update-slice_fusion.2
  1129.4 1.8 dynamic-slice_select_fusion.2
  1131.2 134.2 %all-gather.2.cloned.1.call-done = bf16[128,256,768]{2,1,0:T(8,128)(2,1)} async-done(((bf16[1,256,768]{2,1,0:T(8,128)(2,1)}), bf16[128,256,768]{2,1,0:T(8,128)(2,1)}) %all-gather.2.cloned.1.call-update) | async-done | bytes 50331664 | tf_op jit(solution)/shard_map/while/body/eval_jaxpr/all_gather | solution.py:9
  1265.4 16.5 %reduce_sum.15 = bf16[256,768]{1,0:T(8,128)(2,1)S(1)} reduce(bf16[128,256,768]{2,1,0:T(8,128)(2,1)} %all-gather.2.cloned.1.call-done, bf16[]{:T(256)} %constant.144.clone.2..sunk), dimensions={0}, to_apply=%region_1.1 | reduce | flops 24969216 | bytes 50724864 | tf_op jit(solution)/shard_map/while/body/eval_jaxpr/reduce_sum | solution.py:9
  1281.9 0.8 bitcast_dynamic-update-slice_fusion.2
  1282.7 4.3 gather_fusion.2
  1287.0 4.3 gather_fusion
  1291.3 6.0 fusion.3
  1297.3 4.8 fusion.7
  1302.2 4.3 gather_fusion.1
  1306.5 4.4 gather_fusion.3
  1310.9 3.3 fusion.5
  1314.3 1.9 slice-done.1
  1316.2 6.7 add_add_fusion
  1322.9 6.7 copy.24
  1329.6 10.5 maximum_convert_fusion
  (49 shorter events, 6.0 us)
Async XLA Ops:
  6.5 1323.0 %copy-start = (bf16[768,768]{1,0:T(8,128)(2,1)S(1)}, bf16[768,768]{1,0:T(8,128)(2,1)}, u32[]{:S(2)}) copy-start(bf16[768,768]{1,0:T(8,128)(2,1)} %param.18) | copy-start | bytes 3538948
  15.1 13.3 copy-start.3
  15.1 13.3 copy-start.5
  16.4 1313.1 %all-to-all-start = ((bf16[128,8,768]{2,1,0:T(8,128)(2,1)}), bf16[128,8,768]{2,1,0:T(8,128)(2,1)}, u32[]{:S(2)}, u32[]{:S(2)}) async-start(bf16[128,8,768]{2,1,0:T(8,128)(2,1)} %bitcast_select_fusion), calls=%async_computation | async-start | bytes 3145728 | tf_op jit(solution)/shard_map/all_to_all | solution.py:58
  28.4 141.8 %all-gather.2.cloned.1.call-start = ((), (), s32[]{:S(2)}) async-start(), calls=%async_computation.1 | async-start | bytes 50724864 | tf_op jit(solution)/shard_map/while/body/eval_jaxpr/all_gather | solution.py:9
  187.5 139.2 %all-gather.2.cloned.1.call-start = ((), (), s32[]{:S(2)}) async-start(), calls=%async_computation.1 | async-start | bytes 50724864 | tf_op jit(solution)/shard_map/while/body/eval_jaxpr/all_gather | solution.py:9
  344.0 139.2 %all-gather.2.cloned.1.call-start = ((), (), s32[]{:S(2)}) async-start(), calls=%async_computation.1 | async-start | bytes 50724864 | tf_op jit(solution)/shard_map/while/body/eval_jaxpr/all_gather | solution.py:9
  500.4 139.2 %all-gather.2.cloned.1.call-start = ((), (), s32[]{:S(2)}) async-start(), calls=%async_computation.1 | async-start | bytes 50724864 | tf_op jit(solution)/shard_map/while/body/eval_jaxpr/all_gather | solution.py:9
  656.9 139.2 %all-gather.2.cloned.1.call-start = ((), (), s32[]{:S(2)}) async-start(), calls=%async_computation.1 | async-start | bytes 50724864 | tf_op jit(solution)/shard_map/while/body/eval_jaxpr/all_gather | solution.py:9
  813.3 139.2 %all-gather.2.cloned.1.call-start = ((), (), s32[]{:S(2)}) async-start(), calls=%async_computation.1 | async-start | bytes 50724864 | tf_op jit(solution)/shard_map/while/body/eval_jaxpr/all_gather | solution.py:9
  969.8 139.2 %all-gather.2.cloned.1.call-start = ((), (), s32[]{:S(2)}) async-start(), calls=%async_computation.1 | async-start | bytes 50724864 | tf_op jit(solution)/shard_map/while/body/eval_jaxpr/all_gather | solution.py:9
  1126.2 139.2 %all-gather.2.cloned.1.call-start = ((), (), s32[]{:S(2)}) async-start(), calls=%async_computation.1 | async-start | bytes 50724864 | tf_op jit(solution)/shard_map/while/body/eval_jaxpr/all_gather | solution.py:9
  1291.3 6.0 copy-start.2
  1306.5 7.8 slice-start
  1310.9 5.3 slice-start.1
  1310.9 5.3 copy-start.1
  1322.9 6.7 copy-start.4
Sparse Core Ops, SparseCore 0:
  33.6 136.6 all-gather.1
  192.7 133.9 all-gather.1
  349.1 133.9 all-gather.1
  505.5 133.9 all-gather.1
  662.0 133.9 all-gather.1
  818.4 133.9 all-gather.1
  974.9 133.9 all-gather.1
  1131.3 133.9 all-gather.1
